TPU v7x, 32 devices: a whole 2x2x4 slice. The times are simulated.
32 devices in a mesh: tp: 2 (over x), rows: 16 (over z, y, core).
Axes of the slice: x: 2, y: 2, z: 4, core: 2. Of those that a mesh axis runs over, the one named last changes fastest.
Arguments:
- patches: bfloat16 [16, 2048, 1152], P('rows', 'tp'), may hold values from -6 to 6
- image_lengths: int32 [16, 4], P('rows'), may hold values from 256 to 1024, as said below
- ln_gain: float32 [2, 1152], replicated, may hold values from 0.5 to 1.5
- ln_bias: float32 [2, 1152], replicated, may hold values from -4 to 4
- query_key_value_weight: bfloat16 [3, 1152, 1152], P(None, 'rows', 'tp'), may hold values from -0.1875 to 0.1875
- out_weight: bfloat16 [1152, 1152], P('rows', 'tp'), may hold values from -1.5 to 1.5
- up_weight: bfloat16 [1152, 4304], P('rows', 'tp'), may hold values from -0.1875 to 0.1875
- down_weight: bfloat16 [1152, 4304], P('rows', 'tp'), may hold values from -0.09375 to 0.09375
- adapter: float32 [2, 55296], P(None, ('tp', 'rows')), may hold values from -0.1875 to 0.1875
- adapter_mean: float32 [2, 55296], P(None, ('tp', 'rows')), may hold values from -3 to 3
- adapter_square: float32 [2, 55296], P(None, ('tp', 'rows')), may hold values from 0.01 to 1
- cotangent: bfloat16 [16, 2048, 1152], P('rows', 'tp'), may hold values from -6 to 6
Outputs:
- output: bfloat16 [16, 2048, 1152], P('rows', 'tp')
- patch_grad: float32 [16, 2048, 1152], P('rows', 'tp')
- adapter_grad: float32 [2, 55296], P(None, ('tp', 'rows'))
- new_adapter: float32 [2, 55296], P(None, ('tp', 'rows'))
- new_mean: float32 [2, 55296], P(None, ('tp', 'rows'))
- new_square: float32 [2, 55296], P(None, ('tp', 'rows'))
Inputs may be any that keep to these rules, and one draw needn't show every extreme that they name: `image_lengths`: each pack holds 4 images laid end to end whose patch counts sum to 2048; in every pack one image has exactly 1024 patches and some image has exactly 256.
All inputs are finite; a program needn't handle non-finite values.
Results may differ from a plain program's by a relative error of at most 0.013.
Values may be sent and summed in bfloat16 or wider, within the bound.
No kernel may reach another device: no remote copies, remote signals or barrier semaphores. Data moves between devices by JAX's collectives and lax.ppermute only.
A program may use at most 256 MiB of HBM per device.

v0:
```python
import math

import jax
import jax.numpy as jnp
from jax import lax
from jax.sharding import PartitionSpec as P

D = 1152
HD = 72
RANK = 16


ln_eps = 1e-06
adapter_scale = 2.0
beta_one = 0.9
beta_two = 0.999
adam_eps = 1e-08
learn_rate = 0.01
decay_rate = 0.01
adam_step = 10.0
gelu_coeff = 0.7978845608028654


def norm_forward(values, gain, shift):
    center = jnp.mean(values, axis=-1, keepdims=True)
    centred = values - center
    inverse = lax.rsqrt(jnp.mean(centred * centred, axis=-1, keepdims=True) + ln_eps)
    scaled = centred * inverse
    return (scaled * gain + shift, scaled, inverse)


def norm_backward(upstream, scaled, inverse, gain):
    weighted = upstream * gain
    mean_grad = jnp.mean(weighted, axis=-1, keepdims=True)
    mean_cross = jnp.mean(weighted * scaled, axis=-1, keepdims=True)
    return inverse * (weighted - mean_grad - scaled * mean_cross)


def gelu_tanh(value):
    return 0.5 * value * (1.0 + jnp.tanh(gelu_coeff * (value + 0.044715 * value * value * value)))


def gelu_slope(value):
    tangent = jnp.tanh(gelu_coeff * (value + 0.044715 * value * value * value))
    return 0.5 * (1.0 + tangent) + 0.5 * value * (1.0 - tangent * tangent) * gelu_coeff * (
        1.0 + 3.0 * 0.044715 * value * value
    )


def masked_scores(query_block, key_heads, segment_block, key_segment):
    scores = jnp.einsum(
        "qhd,khd->hqk", query_block, key_heads, preferred_element_type=jnp.float32
    ) * HD ** (-0.5)
    same_image = segment_block[:, None] == key_segment[None, :]
    return jnp.where(same_image[None], scores, -jnp.inf)


def attention_forward(query, keys, values, query_segment, key_segment):
    length = query.shape[0]
    key_len = keys.shape[0]
    heads = query.shape[1] // HD
    block = min(512, length)
    blocks = length // block
    query_heads = query.reshape(blocks, block, heads, HD)
    key_heads = keys.reshape(key_len, heads, HD)
    value_heads = values.reshape(key_len, heads, HD)

    def one_block(inputs):
        query_block, segment_block = inputs
        scores = masked_scores(query_block, key_heads, segment_block, key_segment)
        highest = jnp.max(scores, axis=-1, keepdims=True)
        weights = jnp.exp(scores - highest)
        totals = jnp.sum(weights, axis=-1, keepdims=True)
        probs = (weights / totals).astype(jnp.bfloat16)
        mixed = jnp.einsum("hqk,khd->qhd", probs, value_heads, preferred_element_type=jnp.float32)
        return (mixed, (highest + jnp.log(totals))[:, :, 0])

    mixed, log_totals = lax.map(one_block, (query_heads, query_segment.reshape(blocks, block)))
    return (mixed.reshape(length, heads * HD), log_totals)


def attention_backward(query, keys, values, query_segment, key_segment, log_totals, upstream):
    length = query.shape[0]
    key_len = keys.shape[0]
    heads = query.shape[1] // HD
    block = min(512, length)
    blocks = length // block
    query_heads = query.reshape(blocks, block, heads, HD)
    key_heads = keys.reshape(key_len, heads, HD)
    value_heads = values.reshape(key_len, heads, HD)
    upstream_heads = upstream.reshape(blocks, block, heads, HD)

    def one_block(carry, inputs):
        key_sum, value_sum = carry
        query_block, segment_block, log_block, upstream_block = inputs
        scores = masked_scores(query_block, key_heads, segment_block, key_segment)
        probs = jnp.exp(scores - log_block[:, :, None])
        grad_probs = jnp.einsum(
            "qhd,khd->hqk", upstream_block, value_heads, preferred_element_type=jnp.float32
        )
        row_inner = jnp.sum(probs * grad_probs, axis=-1, keepdims=True)
        grad_scores = (probs * (grad_probs - row_inner)).astype(jnp.bfloat16)
        grad_query = jnp.einsum(
            "hqk,khd->qhd", grad_scores, key_heads, preferred_element_type=jnp.float32
        ) * HD ** (-0.5)
        key_part = jnp.einsum(
            "hqk,qhd->khd", grad_scores, query_block, preferred_element_type=jnp.float32
        ) * HD ** (-0.5)
        value_part = jnp.einsum(
            "hqk,qhd->khd",
            probs.astype(jnp.bfloat16),
            upstream_block,
            preferred_element_type=jnp.float32,
        )
        return ((key_sum + key_part, value_sum + value_part), grad_query)

    empty = jnp.zeros((key_len, heads, HD), jnp.float32)
    (key_sum, value_sum), grad_query = lax.scan(
        one_block,
        (empty, empty),
        (query_heads, query_segment.reshape(blocks, block), log_totals, upstream_heads),
    )
    width = heads * HD
    return (
        grad_query.reshape(length, width).astype(jnp.bfloat16),
        key_sum.reshape(key_len, width),
        value_sum.reshape(key_len, width),
    )


def heads_flow(
    local_values,
    upstream_local,
    segment,
    head_start,
    local_len,
    weights,
    downs,
    up_adapters,
    ln_gain,
    ln_bias,
):
    qkv_all, out_all, up_all, down_all = weights
    heads_width = qkv_all.shape[2]
    ups_local = lax.dynamic_slice_in_dim(up_adapters, head_start, heads_width, 1)
    first_normed, scaled_one, inverse_one = norm_forward(local_values, ln_gain[0], ln_bias[0])
    first_rows = lax.all_gather(first_normed.astype(jnp.bfloat16), "tp", axis=0, tiled=True)
    inner_product = []
    projected = []
    for slot_index in range(3):
        inner_now = jnp.dot(
            first_rows, downs[slot_index], preferred_element_type=jnp.float32
        ).astype(jnp.bfloat16)
        complete_rows = jnp.dot(first_rows, qkv_all[slot_index], preferred_element_type=jnp.float32)
        complete_rows = complete_rows + adapter_scale * jnp.einsum(
            "cr,hr->ch", inner_now, ups_local[slot_index], preferred_element_type=jnp.float32
        )
        inner_product.append(inner_now)
        projected.append(complete_rows.astype(jnp.bfloat16))
    attended, log_totals = attention_forward(
        projected[0], projected[1], projected[2], segment, segment
    )
    attended = attended.astype(jnp.bfloat16)
    piece = attended
    mixed = local_values + lax.psum_scatter(
        jnp.einsum("ch,dh->cd", piece, out_all[0], preferred_element_type=jnp.float32),
        "tp",
        scatter_dimension=0,
        tiled=True,
    )
    normed_two, scaled_two, inverse_two = norm_forward(mixed, ln_gain[1], ln_bias[1])
    second_rows = lax.all_gather(normed_two.astype(jnp.bfloat16), "tp", axis=0, tiled=True)
    hidden = jnp.dot(second_rows, up_all[0], preferred_element_type=jnp.float32)
    active = gelu_tanh(hidden).astype(jnp.bfloat16)
    piece = active
    output = (
        mixed
        + lax.psum_scatter(
            jnp.einsum("cf,df->cd", piece, down_all[0], preferred_element_type=jnp.float32).astype(
                jnp.bfloat16
            ),
            "tp",
            scatter_dimension=0,
            tiled=True,
        ).astype(jnp.float32)
    ).astype(jnp.bfloat16)
    upstream_all = lax.all_gather(upstream_local, "tp", axis=0, tiled=True)
    grad_active = jnp.dot(upstream_all, down_all[0], preferred_element_type=jnp.float32)
    grad_hidden = (grad_active * gelu_slope(hidden)).astype(jnp.bfloat16)
    piece = grad_hidden
    grad_normed_two = lax.psum_scatter(
        jnp.einsum("cf,df->cd", piece, up_all[0], preferred_element_type=jnp.float32),
        "tp",
        scatter_dimension=0,
        tiled=True,
    )
    grad_mixed = upstream_local.astype(jnp.float32) + norm_backward(
        grad_normed_two, scaled_two, inverse_two, ln_gain[1]
    )
    grad_mixed_all = lax.all_gather(grad_mixed.astype(jnp.bfloat16), "tp", axis=0, tiled=True)
    grad_attended = jnp.dot(grad_mixed_all, out_all[0], preferred_element_type=jnp.float32).astype(
        jnp.bfloat16
    )
    grad_query, key_sum, value_sum = attention_backward(
        projected[0], projected[1], projected[2], segment, segment, log_totals, grad_attended
    )
    grads = (grad_query, key_sum.astype(jnp.bfloat16), value_sum.astype(jnp.bfloat16))
    summed_total = jnp.zeros((local_len * lax.axis_size("tp"), D), jnp.float32)
    for input_slot_index in range(3):
        piece = grads[input_slot_index]
        summed_total = summed_total + jnp.einsum(
            "ch,dh->cd", piece, qkv_all[input_slot_index], preferred_element_type=jnp.float32
        )
        through = jnp.dot(piece, ups_local[input_slot_index], preferred_element_type=jnp.float32)
        summed_total = summed_total + adapter_scale * jnp.dot(
            through, downs[input_slot_index].astype(jnp.float32).T, precision=lax.Precision.HIGHEST
        )
    grad_normed_one = lax.psum_scatter(
        summed_total.astype(jnp.bfloat16), "tp", scatter_dimension=0, tiled=True
    ).astype(jnp.float32)
    patch_grad = grad_mixed + norm_backward(grad_normed_one, scaled_one, inverse_one, ln_gain[0])
    down_parts = []
    up_parts = []
    for slot_index in range(3):
        cross = jnp.einsum(
            "cd,ch->dh", first_rows, grads[slot_index], preferred_element_type=jnp.float32
        )
        down_parts.append(
            adapter_scale
            * jnp.dot(
                cross, ups_local[slot_index].astype(jnp.float32), precision=lax.Precision.HIGHEST
            )
        )
        up_parts.append(
            adapter_scale
            * jnp.einsum(
                "ch,cr->hr",
                grads[slot_index],
                inner_product[slot_index],
                preferred_element_type=jnp.float32,
            )
        )
    down_grad = jnp.stack(down_parts)
    up_grad = lax.dynamic_update_slice_in_dim(
        jnp.zeros((3, D, RANK), jnp.float32), jnp.stack(up_parts), head_start, 1
    )
    local_grad = jnp.stack([down_grad.reshape(-1), up_grad.reshape(-1)])
    return (output, patch_grad, local_grad)


def shards(
    patches,
    image_lengths,
    ln_gain,
    ln_bias,
    query_key_value_weight,
    out_weight,
    up_weight,
    down_weight,
    adapter,
    adapter_mean,
    adapter_square,
    cotangent,
):
    tp_count = lax.axis_size("tp")
    tp_index = lax.axis_index("tp")
    local_values = patches[0].astype(jnp.float32)
    local_len = local_values.shape[0]
    pack = local_len * tp_count
    adapter_all = lax.all_gather(adapter.astype(jnp.bfloat16), ("tp", "rows"), axis=1, tiled=True)
    downs = adapter_all[0].reshape(3, D, RANK)
    up_adapters = adapter_all[1].reshape(3, D, RANK)
    weights = (
        lax.all_gather(query_key_value_weight, "rows", axis=1, tiled=True),
        lax.all_gather(out_weight[None], "rows", axis=1, tiled=True),
        lax.all_gather(up_weight[None], "rows", axis=1, tiled=True),
        lax.all_gather(down_weight[None], "rows", axis=1, tiled=True),
    )
    ends = jnp.cumsum(image_lengths[0], dtype=jnp.int32)
    positions = lax.iota(jnp.int32, pack)
    segment = jnp.sum((positions[:, None] >= ends[None, :]).astype(jnp.int32), axis=1)
    head_start = tp_index * query_key_value_weight.shape[2]
    output, patch_grad, local_grad = heads_flow(
        local_values,
        cotangent[0],
        segment,
        head_start,
        local_len,
        weights,
        downs,
        up_adapters,
        ln_gain,
        ln_bias,
    )
    summed_grad = lax.psum_scatter(local_grad, ("tp", "rows"), scatter_dimension=1, tiled=True)
    adapter_grad = summed_grad / math.sqrt(lax.axis_size("rows") * pack)
    new_mean = beta_one * adapter_mean + (1.0 - beta_one) * adapter_grad
    new_square = beta_two * adapter_square + (1.0 - beta_two) * adapter_grad * adapter_grad
    fixed_mean = new_mean / (1.0 - beta_one**adam_step)
    fixed_square = new_square / (1.0 - beta_two**adam_step)
    new_adapter = adapter - learn_rate * (
        fixed_mean / (jnp.sqrt(fixed_square) + adam_eps) + decay_rate * adapter
    )
    return (output[None], patch_grad[None], adapter_grad, new_adapter, new_mean, new_square)


def solution(mesh):
    in_specs = (
        P("rows", "tp", None),
        P("rows", None),
        P(),
        P(),
        P(None, "rows", "tp"),
        P("rows", "tp"),
        P("rows", "tp"),
        P("rows", "tp"),
        P(None, ("tp", "rows")),
        P(None, ("tp", "rows")),
        P(None, ("tp", "rows")),
        P("rows", "tp", None),
    )
    out_specs = (
        P("rows", "tp", None),
        P("rows", "tp", None),
        P(None, ("tp", "rows")),
        P(None, ("tp", "rows")),
        P(None, ("tp", "rows")),
        P(None, ("tp", "rows")),
    )
    return jax.shard_map(shards, mesh=mesh, in_specs=in_specs, out_specs=out_specs, check_vma=False)
```

profile of v0, /device:TPU:0, one launch (start us, length us, event | category | flops | bytes accessed | tf_op | source)
XLA Modules:
  0.0 1848.6 jit_solution(10866068834653989048)
XLA Ops:
  17.1 44.6 %all-gather.4 = bf16[32,1728,2]{1,2,0:T(2,128)(2,1)S(1)} all-gather(bf16[1,1728,2]{1,2,0:T(2,128)(2,1)S(1)} %convert_bitcast_fusion.1), channel_id=1, replica_groups=mesh['tp'=2,'rows'=16] {'tp','rows'}, dimensions={0}, use_global_device_ids=true | all-gather | bytes 228096 | tf_op jit(solution)/shard_map/all_gather | solution.py:270
  87.6 47.4 %all-gather.16.cloned.1.call-done = bf16[3,1152,576]{2,1,0:T(8,128)(2,1)} async-done(((bf16[3,72,576]{2,1,0:T(8,128)(2,1)}), bf16[3,1152,576]{2,1,0:T(8,128)(2,1)}) %all-gather.16.cloned.1.call-update) | async-done | bytes 3981328 | tf_op jit(solution)/shard_map/all_gather | solution.py:274
  165.1 187.9 %while.27 = (s32[]{:T(128)}, bf16[4,512,8,72]{1,3,2,0:T(8,128)(2,1)}, f32[4,8,512]{2,1,0:T(8,128)}, s32[4,512]{1,0:T(4,128)S(1)}, s32[2048]{0:T(1024)S(1)}, /*in...) while((s32[]{:T(128)}, ...), condition=%wide.region_7.8_spmd, body=%wide.region_4.7_spmd.sunk | while | flops 2517626880 | bytes 111492704 | solution.py:78
  370.2 108.6 %reduce-scatter.8.cloned.1.call-done = f32[1024,1152]{1,0:T(8,128)} async-done(((f32[2048,1152]{1,0:T(8,128)}), f32[1024,1152]{1,0:T(8,128)}) %reduce-scatter.8.cloned.1.call-update) | async-done | bytes 4718608 | tf_op jit(solution)/shard_map/reduce_scatter | solution.py:165
  487.6 48.1 %all-gather.24.cloned.1.call-done = bf16[1152,2152]{1,0:T(8,128)(2,1)} async-done(((bf16[72,2152]{1,0:T(8,128)(2,1)}), bf16[1152,2152]{1,0:T(8,128)(2,1)}) %all-gather.24.cloned.1.call-update) | async-done | bytes 4958224 | tf_op jit(solution)/shard_map/all_gather | solution.py:276
  535.7 63.2 %all-gather.18.cloned.1.call-done = bf16[2048,1152]{1,0:T(8,128)(2,1)} async-done(((bf16[1024,1152]{1,0:T(8,128)(2,1)}), bf16[2048,1152]{1,0:T(8,128)(2,1)}) %all-gather.18.cloned.1.call-update) | async-done | bytes 4718608 | tf_op jit(solution)/shard_map/all_gather | solution.py:172
  617.8 45.3 %all-gather.28.cloned.1.call-done = bf16[1,2048,1152]{2,1,0:T(8,128)(2,1)} async-done(((bf16[1,1024,1152]{2,1,0:T(8,128)(2,1)}), bf16[1,2048,1152]{2,1,0:T(8,128)(2,1)}) %all-gather.28.cloned.1.call-update) | async-done | bytes 4718608 | tf_op jit(solution)/shard_map/all_gather | solution.py:187
  663.2 57.1 %all-gather.26.cloned.1.call-done = bf16[1152,2152]{1,0:T(8,128)(2,1)} async-done(((bf16[72,2152]{1,0:T(8,128)(2,1)}), bf16[1152,2152]{1,0:T(8,128)(2,1)}) %all-gather.26.cloned.1.call-update) | async-done | bytes 4958224 | tf_op jit(solution)/shard_map/all_gather | solution.py:277
  720.3 40.5 %fusion.42 = f32[2048,1152]{1,0:T(8,128)} fusion(bf16[1152,2152]{1,0:T(8,128)(2,1)} %all-gather.24.cloned.1.call-done, f32[2048,2152]{0,1:T(8,128)} %fusion.103, bf16[1152,2152]{1,0:T(8,128)(2,1)} %all-gather.26.cloned.1.call-done, bf16[1,2048,1152]{2,1,0:T(8,128)(2,1)} %all-gather.28.cloned.1.call-done), kind=kOutput, calls=%fused_computation.61 | convolution fusion | flops 20392558592 | bytes 41701376 | tf_op jit(solution)/shard_map/cf,df->cd/dot_general | solution.py:192
  760.8 22.9 %fusion.45 = bf16[2048,1152]{1,0:T(8,128)(2,1)} fusion(bf16[1152,2152]{1,0:T(8,128)(2,1)} %all-gather.26.cloned.1.call-done, f32[2048,2152]{0,1:T(8,128)} %fusion.103), kind=kOutput, calls=%fused_computation.64 | convolution fusion | flops 10196434944 | bytes 27305984 | tf_op jit(solution)/shard_map/cf,df->cd/dot_general | solution.py:179
  783.9 86.2 %reduce-scatter.12.cloned.1.call-done = f32[1024,1152]{1,0:T(8,128)} async-done(((f32[2048,1152]{1,0:T(8,128)}), f32[1024,1152]{1,0:T(8,128)}) %reduce-scatter.12.cloned.1.call-update) | async-done | bytes 4718608 | tf_op jit(solution)/shard_map/reduce_scatter | solution.py:191
  874.6 57.6 %reduce-scatter.10.cloned.1.call-done = bf16[1024,1152]{1,0:T(8,128)(2,1)} async-done(((bf16[2048,1152]{1,0:T(8,128)(2,1)}), bf16[1024,1152]{1,0:T(8,128)(2,1)}) %reduce-scatter.10.cloned.1.call-update) | async-done | bytes 2359312 | tf_op jit(solution)/shard_map/reduce_scatter | solution.py:178
  939.9 62.7 %all-gather.20.cloned.1.call-done = bf16[2048,1152]{1,0:T(8,128)(2,1)} async-done(((bf16[1024,1152]{1,0:T(8,128)(2,1)}), bf16[2048,1152]{1,0:T(8,128)(2,1)}) %all-gather.20.cloned.1.call-update) | async-done | bytes 4718608 | tf_op jit(solution)/shard_map/all_gather | solution.py:200
  1017.0 439.4 %while.28 = (s32[]{:T(128)}, f32[2048,8,72]{0,2,1:T(8,128)}, f32[2048,8,72]{0,2,1:T(8,128)}, bf16[4,512,8,72]{1,3,2,0:T(8,128)(2,1)}, bf16[4,512,8,72]{1,3,2,0:T...) while((s32[]{:T(128)}, f32[2048,8,72]{0,2,1:T(8,128)}, ...), condition=%wide.region_17.18_spmd.clone, body=%wide.region_15.17_spmd.clone.sunk | while | flops 6122532864 | bytes 359891648 | solution.py:118
  1036.7 24.7 %multiply_reduce_fusion.5 = (f32[8,512]{1,0:T(8,128)S(1)}, f32[8,512,2048]{2,1,0:T(8,128)}) fusion(f32[8,512,2048]{2,1,0:T(8,128)} %fusion.192, f32[8,512]{1,0:T(8,128)S(1)} %dynamic-slice_bitcast_fusion.14, bf16[2048,8,72]{0,2,1:T(8,128)(2,1)S(1)} %get-tuple-element.473, bf16[4,512,8,72]{1,3,2,0:T(8,128)(2,1)} %get-tuple-element.470, ...), kind=kOutput, calls=%fused_computation.18.clone.1 | convolution fusion | flops 1249898496 | bytes 71139840 | tf_op jit(solution)/shard_map/while/body/eval_jaxpr/qhd,khd->hqk/dot_general | solution.py:51
  1061.5 27.5 %multiply_convert_fusion.6 = bf16[8,512,2048]{2,1,0:T(8,128)(2,1)} fusion(f32[8,512,2048]{2,1,0:T(8,128)} %get-tuple-element.411, f32[8,512,2048]{2,1,0:T(8,128)} %fusion.192, f32[8,512]{1,0:T(8,128)S(1)} %get-tuple-element.412), kind=kLoop, calls=%fused_computation.17.clone.1 | loop fusion | flops 25165824 | bytes 83902464 | tf_op jit(solution)/shard_map/while/body/eval_jaxpr/convert_element_type | solution.py:102
  1144.5 24.7 %multiply_reduce_fusion.5 = (f32[8,512]{1,0:T(8,128)S(1)}, f32[8,512,2048]{2,1,0:T(8,128)}) fusion(f32[8,512,2048]{2,1,0:T(8,128)} %fusion.192, f32[8,512]{1,0:T(8,128)S(1)} %dynamic-slice_bitcast_fusion.14, bf16[2048,8,72]{0,2,1:T(8,128)(2,1)S(1)} %get-tuple-element.473, bf16[4,512,8,72]{1,3,2,0:T(8,128)(2,1)} %get-tuple-element.470, ...), kind=kOutput, calls=%fused_computation.18.clone.1 | convolution fusion | flops 1249898496 | bytes 71139840 | tf_op jit(solution)/shard_map/while/body/eval_jaxpr/qhd,khd->hqk/dot_general | solution.py:51
  1169.2 27.5 %multiply_convert_fusion.6 = bf16[8,512,2048]{2,1,0:T(8,128)(2,1)} fusion(f32[8,512,2048]{2,1,0:T(8,128)} %get-tuple-element.411, f32[8,512,2048]{2,1,0:T(8,128)} %fusion.192, f32[8,512]{1,0:T(8,128)S(1)} %get-tuple-element.412), kind=kLoop, calls=%fused_computation.17.clone.1 | loop fusion | flops 25165824 | bytes 83902464 | tf_op jit(solution)/shard_map/while/body/eval_jaxpr/convert_element_type | solution.py:102
  1254.9 24.7 %multiply_reduce_fusion.5 = (f32[8,512]{1,0:T(8,128)S(1)}, f32[8,512,2048]{2,1,0:T(8,128)}) fusion(f32[8,512,2048]{2,1,0:T(8,128)} %fusion.192, f32[8,512]{1,0:T(8,128)S(1)} %dynamic-slice_bitcast_fusion.14, bf16[2048,8,72]{0,2,1:T(8,128)(2,1)S(1)} %get-tuple-element.473, bf16[4,512,8,72]{1,3,2,0:T(8,128)(2,1)} %get-tuple-element.470, ...), kind=kOutput, calls=%fused_computation.18.clone.1 | convolution fusion | flops 1249898496 | bytes 71139840 | tf_op jit(solution)/shard_map/while/body/eval_jaxpr/qhd,khd->hqk/dot_general | solution.py:51
  1279.6 27.5 %multiply_convert_fusion.6 = bf16[8,512,2048]{2,1,0:T(8,128)(2,1)} fusion(f32[8,512,2048]{2,1,0:T(8,128)} %get-tuple-element.411, f32[8,512,2048]{2,1,0:T(8,128)} %fusion.192, f32[8,512]{1,0:T(8,128)S(1)} %get-tuple-element.412), kind=kLoop, calls=%fused_computation.17.clone.1 | loop fusion | flops 25165824 | bytes 83902464 | tf_op jit(solution)/shard_map/while/body/eval_jaxpr/convert_element_type | solution.py:102
  1365.2 24.7 %multiply_reduce_fusion.5 = (f32[8,512]{1,0:T(8,128)S(1)}, f32[8,512,2048]{2,1,0:T(8,128)}) fusion(f32[8,512,2048]{2,1,0:T(8,128)} %fusion.192, f32[8,512]{1,0:T(8,128)S(1)} %dynamic-slice_bitcast_fusion.14, bf16[2048,8,72]{0,2,1:T(8,128)(2,1)S(1)} %get-tuple-element.473, bf16[4,512,8,72]{1,3,2,0:T(8,128)(2,1)} %get-tuple-element.470, ...), kind=kOutput, calls=%fused_computation.18.clone.1 | convolution fusion | flops 1249898496 | bytes 71139840 | tf_op jit(solution)/shard_map/while/body/eval_jaxpr/qhd,khd->hqk/dot_general | solution.py:51
  1390.0 27.5 %multiply_convert_fusion.6 = bf16[8,512,2048]{2,1,0:T(8,128)(2,1)} fusion(f32[8,512,2048]{2,1,0:T(8,128)} %get-tuple-element.411, f32[8,512,2048]{2,1,0:T(8,128)} %fusion.192, f32[8,512]{1,0:T(8,128)S(1)} %get-tuple-element.412), kind=kLoop, calls=%fused_computation.17.clone.1 | loop fusion | flops 25165824 | bytes 83902464 | tf_op jit(solution)/shard_map/while/body/eval_jaxpr/convert_element_type | solution.py:102
  1558.4 213.1 %reduce-scatter.16.cloned.1.call-done = f32[1728,2]{1,0:T(8,128)} async-done(((f32[55296,2]{1,0:T(8,128)}), f32[1728,2]{1,0:T(8,128)}) %reduce-scatter.16.cloned.1.call-update) | async-done | bytes 13840
  1773.7 59.9 %reduce-scatter.14.cloned.1.call-done = bf16[1024,1152]{1,0:T(8,128)(2,1)} async-done(((bf16[2048,1152]{1,0:T(8,128)(2,1)}), bf16[1024,1152]{1,0:T(8,128)(2,1)}) %reduce-scatter.14.cloned.1.call-update) | async-done | bytes 2359312 | tf_op jit(solution)/shard_map/reduce_scatter | solution.py:218
  (296 shorter events, 666.3 us)
Async XLA Ops:
  7.2 73.9 %all-gather.14.cloned.1.call-start = ((), (), s32[]{:S(2)}) async-start(), calls=%async_computation.5 | async-start | bytes 7077888 | tf_op jit(solution)/shard_map/all_gather | solution.py:147
  15.6 119.5 %all-gather.16.cloned.1.call-start = ((), (), s32[]{:S(2)}) async-start(), calls=%async_computation.6 | async-start | bytes 4700160 | tf_op jit(solution)/shard_map/all_gather | solution.py:274
  16.3 343.2 %all-gather.22.cloned.1.call-start = ((), (), s32[]{:S(2)}) async-start(), calls=%async_computation.13 | async-start | bytes 1566720 | tf_op jit(solution)/shard_map/all_gather | solution.py:275
  17.1 461.7 %reduce-scatter.8.cloned.1.call-start = ((), (), s32[]{:S(2)}) async-start(), calls=%async_computation.7 | async-start | bytes 14155776 | tf_op jit(solution)/shard_map/reduce_scatter | solution.py:165
  64.2 97.1 %copy-start.15 = (bf16[3,1152,16]{2,1,0:T(8,128)(2,1)}, bf16[3,1152,16]{2,1,0:T(8,128)(2,1)S(1)}, u32[]{:S(2)}) copy-start(bf16[3,1152,16]{2,1,0:T(8,128)(2,1)S(1)} %reshape_squeeze.4) | copy-start | bytes 331780
  86.3 75.1 %copy-start.26 = (bf16[2048,16]{0,1:T(8,128)(2,1)}, bf16[2048,16]{0,1:T(8,128)(2,1)S(1)}, u32[]{:S(2)}) copy-start(bf16[2048,16]{0,1:T(8,128)(2,1)S(1)} %convolution_convert_fusion.1) | copy-start | bytes 196612
  369.5 109.2 %copy-start.7 = (bf16[1,1024,1152]{2,1,0:T(8,128)(2,1)S(1)}, bf16[1,1024,1152]{2,1,0:T(8,128)(2,1)}, u32[]{:S(2)}) copy-start(bf16[1,1024,1152]{2,1,0:T(8,128)(2,1)} %param.16) | copy-start | bytes 7077892
  369.5 166.2 %all-gather.24.cloned.1.call-start = ((), (), s32[]{:S(2)}) async-start(), calls=%async_computation.14 | async-start | bytes 5326848 | tf_op jit(solution)/shard_map/all_gather | solution.py:276
  370.1 228.8 %all-gather.18.cloned.1.call-start = ((), (), s32[]{:S(2)}) async-start(), calls=%async_computation.8 | async-start | bytes 7077888 | tf_op jit(solution)/shard_map/all_gather | solution.py:172
  486.1 177.1 %all-gather.28.cloned.1.call-start = ((), (), s32[]{:S(2)}) async-start(), calls=%async_computation.16 | async-start | bytes 7077888 | tf_op jit(solution)/shard_map/all_gather | solution.py:187
  486.8 233.5 %all-gather.26.cloned.1.call-start = ((), (), s32[]{:S(2)}) async-start(), calls=%async_computation.15 | async-start | bytes 5326848 | tf_op jit(solution)/shard_map/all_gather | solution.py:277
  487.6 382.5 %reduce-scatter.12.cloned.1.call-start = ((), (), s32[]{:S(2)}) async-start(), calls=%async_computation.10 | async-start | bytes 14155776 | tf_op jit(solution)/shard_map/reduce_scatter | solution.py:191
  760.8 171.4 %reduce-scatter.10.cloned.1.call-start = ((), (), s32[]{:S(2)}) async-start(), calls=%async_computation.9 | async-start | bytes 7077888 | tf_op jit(solution)/shard_map/reduce_scatter | solution.py:178
  783.8 148.4 %copy-start.13 = (bf16[1,1024,1152]{2,1,0:T(8,128)(2,1)S(1)}, bf16[1,1024,1152]{2,1,0:T(8,128)(2,1)}, u32[]{:S(2)}) copy-start(bf16[1,1024,1152]{2,1,0:T(8,128)(2,1)} %param.27) | copy-start | bytes 7077892
  783.8 218.8 %all-gather.20.cloned.1.call-start = ((), (), s32[]{:S(2)}) async-start(), calls=%async_computation.11 | async-start | bytes 7077888 | tf_op jit(solution)/shard_map/all_gather | solution.py:200
  939.8 831.8 %reduce-scatter.16.cloned.1.call-start = ((), (), s32[]{:S(2)}) async-start(), calls=%async_computation.17 | async-start | bytes 29196288
  1507.7 326.0 %reduce-scatter.14.cloned.1.call-start = ((), (), s32[]{:S(2)}) async-start(), calls=%async_computation.12 | async-start | bytes 7077888 | tf_op jit(solution)/shard_map/reduce_scatter | solution.py:218
  1558.4 214.7 %copy-start.41 = (f32[2,1728]{1,0:T(2,128)S(1)}, f32[2,1728]{1,0:T(2,128)}, u32[]{:S(2)}) copy-start(f32[2,1728]{1,0:T(2,128)} %param.24) | copy-start | bytes 41476
  1558.4 214.7 %copy-start.43 = (f32[2,1728]{1,0:T(2,128)S(1)}, f32[2,1728]{1,0:T(2,128)}, u32[]{:S(2)}) copy-start(f32[2,1728]{1,0:T(2,128)} %param.25) | copy-start | bytes 41476
  1558.4 214.7 %copy-start.44 = (f32[2,1728]{1,0:T(2,128)S(1)}, f32[2,1728]{1,0:T(2,128)}, u32[]{:S(2)}) copy-start(f32[2,1728]{1,0:T(2,128)} %param.26) | copy-start | bytes 41476
  1558.4 275.3 %copy-start.8 = (bf16[1,1024,1152]{2,1,0:T(8,128)(2,1)S(1)}, bf16[1,1024,1152]{2,1,0:T(8,128)(2,1)}, u32[]{:S(2)}) copy-start(bf16[1,1024,1152]{2,1,0:T(8,128)(2,1)} %param.16) | copy-start | bytes 7077892
  1558.4 275.3 %copy-start.33 = (f32[1152]{0:T(1024)S(1)}, f32[1152]{0:T(1024)}, u32[]{:S(2)}) copy-start(f32[1152]{0:T(1024)} %copy-done.32) | copy-start | bytes 13828
  1558.4 275.3 %copy-start.36 = (f32[1024]{0:T(1024)S(1)}, f32[1024]{0:T(1024)}, u32[]{:S(2)}) copy-start(f32[1024]{0:T(1024)} %copy-done.35) | copy-start | bytes 12292
  1558.4 275.2 %copy-start.39 = (f32[1024]{0:T(1024)S(1)}, f32[1024]{0:T(1024)}, u32[]{:S(2)}) copy-start(f32[1024]{0:T(1024)} %copy-done.38) | copy-start | bytes 12292
  (51 other events, 546.9 us)
Sparse Core Ops, SparseCore 0:
  15.7 65.3 all-gather.13
  83.3 51.7 all-gather.15
  137.2 37.8 all-gather.21
  369.7 109.0 reduce-scatter.7
  480.8 54.9 all-gather.23
  537.7 61.1 all-gather.17
  600.5 62.6 all-gather.27
  665.3 54.9 all-gather.25
  760.9 109.0 reduce-scatter.11
  872.2 59.9 reduce-scatter.9
  939.9 62.6 all-gather.19
  1507.8 263.7 reduce-scatter.15
  1774.0 59.6 reduce-scatter.13
where the time goes:
time: 1860 us; the launch traced here: 1850 us
  waiting for transfers between devices  869 us (47%)
  matrix products  634 us (34%)
  other arithmetic  214 us (12%)
  local copies, waits for them, and re-layouts  70.1 us (4%)
  blocking collectives  44.6 us (2%)
    unnamed x14, waiting for transfers between devices  217 us
    dot_general x8, matrix products, masked_scores(): jnp.einsum('qhd,khd->hqk', query_block, key_heads, preferred_element_type...  159 us
    convert_element_type x4, other arithmetic, one_block(): grad_scores = (probs * (grad_probs - row_inner)).astype(jnp.bfloat16)  110 us
    reduce_scatter x1, waiting for transfers between devices, heads_flow(): lax.psum_scatter(jnp.einsum('ch,dh->cd', piece, out_all[0], preferred_ele...  109 us
    reduce_scatter x1, waiting for transfers between devices, heads_flow(): lax.psum_scatter(jnp.einsum('cf,df->cd', piece, up_all[0], preferred_elem...  86.2 us
    dot_general x4, matrix products, one_block(): jnp.einsum('qhd,khd->hqk', upstream_block, value_heads, preferred_element...  69.9 us
    dot_general x4, matrix products, one_block(): jnp.einsum('hqk,qhd->khd', probs.astype(jnp.bfloat16), upstream_block, pr...  68.7 us
    all_gather x1, waiting for transfers between devices, heads_flow(): lax.all_gather(normed_two.astype(jnp.bfloat16), 'tp', axis=0, tiled=True)  63.2 us
  transfers between devices with their start and end apart: 13, of which 12 were waited for; matrix products, arithmetic and copies ran while one was open for 18% of the time, Pallas kernels for 0%

commit v1 on v0

v1 whole, which is shorter than its diff:
```python
import functools
import math

import jax
import jax.numpy as jnp
from jax import lax
from jax.experimental import pallas as pl
from jax.experimental.pallas import tpu as pltpu
from jax.sharding import PartitionSpec as P

HD = 72
RANK = 16
LANES = 128

ln_eps = 1e-06
adapter_scale = 2.0
beta_one = 0.9
beta_two = 0.999
adam_eps = 1e-08
learn_rate = 0.01
decay_rate = 0.01
adam_step = 10.0
gelu_coeff = 0.7978845608028654
log2_e = 1.4426950408889634
score_scale = HD ** (-0.5)

f32 = jnp.float32
bf16 = jnp.bfloat16
VMEM_LIMIT = 60 * 2**20


def dot(left, right, left_dim, right_dim):
    return lax.dot_general(
        left, right, (((left_dim,), (right_dim,)), ((), ())), preferred_element_type=f32
    )


def call(kernel, grid, in_specs, out_specs, out_shape, scratch=()):
    return pl.pallas_call(
        kernel,
        grid=grid,
        in_specs=in_specs,
        out_specs=out_specs,
        out_shape=out_shape,
        scratch_shapes=list(scratch),
        compiler_params=pltpu.CompilerParams(vmem_limit_bytes=VMEM_LIMIT),
    )


def whole(shape):
    return pl.BlockSpec(shape, lambda *_: (0,) * len(shape))


def struct(shape, dtype):
    return jax.ShapeDtypeStruct(shape, dtype)


def lane_loop(count, body):
    def step(i, carry):
        body(pl.ds(pl.multiple_of(i * LANES, LANES), LANES))
        return carry

    lax.fori_loop(0, count // LANES, step, 0)


def project_kernel(qkv_width, x_ref, gain_ref, shift_ref, downs_ref, ups_ref, w_ref,
                   qkv_ref, xt_ref, normed_ref, inner_ref):
    length = x_ref.shape[0]

    @pl.when(pl.program_id(0) == 0)
    def _():
        def norm(at):
            v = x_ref[at, :].astype(f32).T
            xt_ref[:, at] = v.astype(bf16)
            centred = v - jnp.mean(v, axis=0, keepdims=True)
            inverse = lax.rsqrt(jnp.mean(centred * centred, axis=0, keepdims=True) + ln_eps)
            normed_ref[:, at] = (centred * inverse * gain_ref[...] + shift_ref[...]).astype(bf16)

        lane_loop(length, norm)
        inner_ref[...] = dot(downs_ref[...], normed_ref[...], 1, 0).astype(bf16)

    width = qkv_width // 3
    acc = dot(w_ref[:, :qkv_width], normed_ref[...], 0, 0)
    acc = acc + adapter_scale * dot(ups_ref[...], inner_ref[...], 0, 0)
    qkv_ref[:width, :] = (acc[:width] * (score_scale * log2_e)).astype(bf16)
    qkv_ref[width:, :] = acc[width:].astype(bf16)


def attend_kernel(q_ref, k_ref, v_ref, seg_col_ref, seg_row_ref, out_ref, probs_ref, inv_ref):
    length = q_ref.shape[1]
    scores = dot(k_ref[...], q_ref[...], 0, 0)
    seg_col = jnp.concatenate([seg_col_ref[...]] * (length // LANES), axis=1)
    scores = jnp.where(seg_col == seg_row_ref[...], scores, -1e30)
    highest = jnp.max(scores, axis=0, keepdims=True)
    weights = jnp.exp2(scores - highest)
    inverse = 1.0 / jnp.sum(weights, axis=0, keepdims=True)
    probs = weights.astype(bf16)
    probs_ref[...] = probs
    inv_ref[...] = inverse
    out_ref[...] = (dot(v_ref[...], probs, 1, 0) * inverse).astype(bf16)


def attend_back_kernel(probs_ref, inv_ref, q_ref, k_ref, v_ref, grad_ref, out_ref,
                       dqkv_ref):
    grad = grad_ref[...].astype(f32) * inv_ref[...]
    delta = jnp.sum(grad * out_ref[...].astype(f32), axis=0, keepdims=True)
    grad = grad.astype(bf16)
    probs = probs_ref[...]
    d_probs = dot(v_ref[...], grad, 0, 0)
    d_scores = (probs.astype(f32) * (d_probs - delta)).astype(bf16)
    dqkv_ref[0] = (dot(k_ref[...], d_scores, 1, 0) * score_scale).astype(bf16)
    dqkv_ref[1] = (dot(q_ref[...], d_scores, 1, 1) * (1.0 / log2_e)).astype(bf16)
    dqkv_ref[2] = dot(grad, probs, 1, 1).astype(bf16)


def mix_kernel(skip, xt_ref, att_ref, w_ref, gain_ref, shift_ref, cot_ref,
               mixed_ref, normed_ref, cot_t_ref, w_buf, padded, sem):
    length = xt_ref.shape[1]
    copies = []
    for t in range(2):
        copies.append(pltpu.make_async_copy(w_ref.at[t, :, pl.ds(w_ref.shape[2] - w_buf.shape[2], w_buf.shape[2])],
                                            w_buf.at[t], sem.at[t]))
        copies[t].start()

    def flip(at):
        cot_t_ref[:, at] = cot_ref[at, :].astype(f32).T.astype(bf16)

    lane_loop(length, flip)
    padded[...] = jnp.zeros_like(padded)
    for t in range(2):
        padded[t, skip:, :] = att_ref[t]
        copies[t].wait()
    mixed_ref[...] = (xt_ref[...].astype(f32) + dot(w_buf[0], padded[0], 1, 0)) + dot(w_buf[1], padded[1], 1, 0)

    def norm(at):
        v = mixed_ref[:, at]
        centred = v - jnp.mean(v, axis=0, keepdims=True)
        inverse = lax.rsqrt(jnp.mean(centred * centred, axis=0, keepdims=True) + ln_eps)
        normed_ref[:, at] = (centred * inverse * gain_ref[...] + shift_ref[...]).astype(bf16)

    lane_loop(length, norm)


def mlp_kernel(normed_ref, cot_ref, up_ref, down_ref, out_ref, grad_ref):
    @pl.when(pl.program_id(0) == 0)
    def _():
        out_ref[...] = jnp.zeros_like(out_ref)
        grad_ref[...] = jnp.zeros_like(grad_ref)

    width = up_ref.shape[1]
    start = 0
    while start < width:
        size = 512 if width - start >= 1024 else width - start
        up = up_ref[:, start : start + size]
        down = down_ref[:, start : start + size]
        hidden = dot(up, normed_ref[...], 0, 0)
        grad_active = dot(down, cot_ref[...], 0, 0)
        square = hidden * hidden
        half = 0.5 + 0.5 * jnp.tanh(hidden * (gelu_coeff + (gelu_coeff * 0.044715) * square))
        active = hidden * half
        slope = half + active * (1.0 - half) * (2.0 * gelu_coeff + (6.0 * 0.044715 * gelu_coeff) * square)
        out_ref[...] += dot(down, active.astype(bf16), 1, 0)
        grad_ref[...] += dot(up, (grad_active * slope).astype(bf16), 1, 0)
        start += size


def turn_kernel(skip, mixed_ref, out_ref, grad_ref, cot_ref, gain_ref, w_ref,
                output_ref, d_mixed_ref, d_att_ref, w_buf, sem):
    length = mixed_ref.shape[1]
    copies = []
    for t in range(2):
        copies.append(pltpu.make_async_copy(w_ref.at[t, :, pl.ds(w_ref.shape[2] - w_buf.shape[2], w_buf.shape[2])],
                                            w_buf.at[t], sem.at[t]))
        copies[t].start()

    def back(at):
        v = mixed_ref[:, at]
        output_ref[at, :] = (v + out_ref[:, at]).T.astype(bf16)
        centred = v - jnp.mean(v, axis=0, keepdims=True)
        inverse = lax.rsqrt(jnp.mean(centred * centred, axis=0, keepdims=True) + ln_eps)
        scaled = centred * inverse
        e = grad_ref[:, at] * gain_ref[...]
        d_norm = inverse * (e - jnp.mean(e, axis=0, keepdims=True)
                            - scaled * jnp.mean(e * scaled, axis=0, keepdims=True))
        d_mixed_ref[:, at] = cot_ref[:, at].astype(f32) + d_norm

    lane_loop(length, back)
    low = d_mixed_ref[...].astype(bf16)
    for t in range(2):
        copies[t].wait()
        d_att_ref[t] = dot(w_buf[t], low, 0, 0)[skip:].astype(bf16)


def finish_kernel(qkv_width, dqkv_ref, w_ref, normed_ref, inner_ref, downs_ref, ups_ref, xt_ref, d_mixed_ref, gain_ref,
                  patch_ref, up_grad_ref, down_grad_ref, total, through):
    length = xt_ref.shape[1]
    first = pl.program_id(0) == 0

    @pl.when(first)
    def _():
        total[...] = jnp.zeros_like(total)
        through[...] = jnp.zeros_like(through)

    total[...] += dot(w_ref[:, :qkv_width], dqkv_ref[...], 1, 0)
    through[...] += dot(ups_ref[...], dqkv_ref[...], 1, 0)
    up_grad_ref[...] = adapter_scale * dot(inner_ref[...], dqkv_ref[...], 1, 1)

    @pl.when(pl.program_id(0) == pl.num_programs(0) - 1)
    def _():
        low = (adapter_scale * through[...]).astype(bf16)
        down_grad_ref[...] = dot(low, normed_ref[...], 1, 1)
        total[...] += dot(downs_ref[...], low, 0, 0)

        def back(at):
            v = xt_ref[:, at].astype(f32)
            centred = v - jnp.mean(v, axis=0, keepdims=True)
            inverse = lax.rsqrt(jnp.mean(centred * centred, axis=0, keepdims=True) + ln_eps)
            scaled = centred * inverse
            e = total[:, at] * gain_ref[...]
            d_norm = inverse * (e - jnp.mean(e, axis=0, keepdims=True)
                                - scaled * jnp.mean(e * scaled, axis=0, keepdims=True))
            patch_ref[at, :] = (d_mixed_ref[:, at] + d_norm).T

        lane_loop(length, back)


def swap(values, use_low, swapped):
    half = values.shape[0] // 2
    window = jnp.where(use_low, values[:half], values[half:])
    other = lax.ppermute(window.astype(bf16), "tp", [(0, 1), (1, 0)])
    return jnp.where(swapped, jnp.concatenate([other, other]).astype(values.dtype), values)


def scatter_sum(value):
    def halve(value, axis_name, bit):
        size = lax.axis_size(axis_name)
        mine = (lax.axis_index(axis_name) // bit) % 2
        kept = lax.dynamic_index_in_dim(value, mine, 0, keepdims=False)
        sent = lax.dynamic_index_in_dim(value, 1 - mine, 0, keepdims=False)
        return kept + lax.ppermute(sent, axis_name, [(i, i ^ bit) for i in range(size)])

    rest = value.shape[1:]
    rows = lax.axis_size("rows")
    value = halve(value.reshape((2, rows) + rest), "tp", 1)
    bit = rows // 2
    while bit:
        value = halve(value.reshape((2, bit) + rest), "rows", bit)
        bit //= 2
    return value[0]


def shards(
    patches,
    image_lengths,
    ln_gain,
    ln_bias,
    query_key_value_weight,
    out_weight,
    up_weight,
    down_weight,
    adapter,
    adapter_mean,
    adapter_square,
    cotangent,
):
    tp_index = lax.axis_index("tp")
    both = ("tp", "rows")
    devices = lax.axis_size("tp") * lax.axis_size("rows")
    length, width = patches.shape[1:]
    depth, part = query_key_value_weight.shape[1:]
    heads = part // HD
    qkv_width = 3 * part
    square_width = 4 * part
    hidden_width = -(-up_weight.shape[1] // LANES) * LANES
    out_width = -(-part // LANES) * LANES
    skip = out_width - part
    own = adapter.shape[1] // RANK

    lengths = image_lengths[0]
    ends = jnp.cumsum(lengths, dtype=jnp.int32)
    start = jnp.sum(jnp.where(lengths == length, ends - lengths, 0))
    use_low = start <= length // 2
    place = lax.iota(jnp.int32, length)
    swapped = jnp.where(use_low, place < start, place >= start)
    position = place + length * jnp.where(swapped, 1 - tp_index, tp_index)
    segment = jnp.sum((position[:, None] >= ends[None, :]).astype(jnp.int32), axis=1)
    seg_col = jnp.broadcast_to(segment[:, None], (length, LANES))
    seg_row = segment[None, :]
    swapped = swapped[:, None]

    x = swap(patches[0], use_low, swapped)
    cot = swap(cotangent[0], use_low, swapped)

    if adapter.shape[1] % RANK == 0:
        local = adapter.astype(bf16).reshape(2, own, RANK).transpose(0, 2, 1)
        every = lax.all_gather(local, both, axis=0)
        every = every.transpose(1, 2, 0, 3).reshape(2, RANK, 3, width).transpose(0, 2, 1, 3)
    else:
        every = lax.all_gather(adapter.astype(bf16), both, axis=0).transpose(1, 0, 2)
        every = every.reshape(2, 3, width, RANK).transpose(0, 1, 3, 2)
    downs = every[0].reshape(3 * RANK, width)
    ups = every[1].reshape(3, RANK, 2, part).transpose(2, 0, 1, 3)
    ups = (ups[:, :, :, None, :] * jnp.eye(3, dtype=bf16)[None, :, None, :, None]).reshape(2, 3 * RANK, qkv_width)

    square = jnp.concatenate([query_key_value_weight[0], query_key_value_weight[1], query_key_value_weight[2], out_weight], axis=1)
    pad = ((0, 0), (0, hidden_width - up_weight.shape[1]))
    square = lax.all_gather(square, both, axis=0, tiled=True).reshape(2, width, square_width)
    up_all = lax.all_gather(jnp.pad(up_weight, pad), both, axis=0, tiled=True).reshape(2, width, hidden_width)
    down_all = lax.all_gather(jnp.pad(down_weight, pad), both, axis=0, tiled=True).reshape(2, width, hidden_width)

    column = lambda v: jnp.broadcast_to(v[:, None], (width, LANES))
    gain_one, gain_two = column(ln_gain[0]), column(ln_gain[1])
    shift_one, shift_two = column(ln_bias[0]), column(ln_bias[1])

    by_part = lambda rows, columns: pl.BlockSpec((None, rows, columns), lambda t: (t, 0, 0))
    qkv, x_t, normed_one, inner = call(
        functools.partial(project_kernel, qkv_width),
        (2,),
        [whole((length, width)), whole((width, LANES)), whole((width, LANES)), whole((3 * RANK, width)),
         by_part(3 * RANK, qkv_width), by_part(width, square_width)],
        [by_part(qkv_width, length), whole((width, length)), whole((width, length)), whole((3 * RANK, length))],
        [struct((2, qkv_width, length), bf16), struct((width, length), bf16), struct((width, length), bf16),
         struct((3 * RANK, length), bf16)],
    )(x, gain_one, shift_one, downs, ups, square)

    qkv = qkv.reshape(2, 3, heads, HD, length)
    head_of = lambda j: pl.BlockSpec((None, None, None, HD, length), lambda t, h: (t, j, h, 0, 0))
    head = pl.BlockSpec((None, None, HD, length), lambda t, h: (t, h, 0, 0))
    table = pl.BlockSpec((None, None, length, length), lambda t, h: (t, h, 0, 0))
    line = pl.BlockSpec((None, None, 1, length), lambda t, h: (t, h, 0, 0))
    attended, probs, inverse = call(
        attend_kernel,
        (2, heads),
        [head_of(0), head_of(1), head_of(2), whole((length, LANES)), whole((1, length))],
        [head, table, line],
        [struct((2, heads, HD, length), bf16), struct((2, heads, length, length), bf16),
         struct((2, heads, 1, length), f32)],
    )(qkv, qkv, qkv, seg_col, seg_row)

    hbm = pl.BlockSpec(memory_space=pl.ANY)
    mixed, normed_two, cot_t = call(
        functools.partial(mix_kernel, skip),
        (1,),
        [whole((width, length)), whole((2, part, length)), hbm, whole((width, LANES)), whole((width, LANES)),
         whole((length, width))],
        [whole((width, length))] * 3,
        [struct((width, length), f32), struct((width, length), bf16), struct((width, length), bf16)],
        [pltpu.VMEM((2, width, out_width), bf16), pltpu.VMEM((2, out_width, length), bf16), pltpu.SemaphoreType.DMA((2,))],
    )(x_t, attended.reshape(2, part, length), square, gain_two, shift_two, cot)

    fed, grad_two = call(
        mlp_kernel,
        (2,),
        [whole((width, length)), whole((width, length)), by_part(width, hidden_width), by_part(width, hidden_width)],
        [whole((width, length))] * 2,
        [struct((width, length), f32)] * 2,
    )(normed_two, cot_t, up_all, down_all)

    output, d_mixed, d_attended = call(
        functools.partial(turn_kernel, skip),
        (1,),
        [whole((width, length))] * 4 + [whole((width, LANES)), hbm],
        [whole((length, width)), whole((width, length)), whole((2, part, length))],
        [struct((length, width), bf16), struct((width, length), f32), struct((2, part, length), bf16)],
        [pltpu.VMEM((2, width, out_width), bf16), pltpu.SemaphoreType.DMA((2,))],
    )(mixed, fed, grad_two, cot_t, gain_two, square)

    three = pl.BlockSpec((None, 3, None, HD, length), lambda t, h: (t, 0, h, 0, 0))
    dqkv = call(
        attend_back_kernel,
        (2, heads),
        [table, line, head_of(0), head_of(1), head_of(2), head, head],
        three,
        struct((2, 3, heads, HD, length), bf16),
    )(probs, inverse, qkv, qkv, qkv, d_attended.reshape(2, heads, HD, length), attended)

    patch_grad, up_grad, down_grad = call(
        functools.partial(finish_kernel, qkv_width),
        (2,),
        [by_part(qkv_width, length), by_part(width, square_width), whole((width, length)), whole((3 * RANK, length)),
         whole((3 * RANK, width)), by_part(3 * RANK, qkv_width), whole((width, length)), whole((width, length)),
         whole((width, LANES))],
        [whole((length, width)), by_part(3 * RANK, qkv_width), whole((3 * RANK, width))],
        [struct((length, width), f32), struct((2, 3 * RANK, qkv_width), f32), struct((3 * RANK, width), f32)],
        [pltpu.VMEM((width, length), f32), pltpu.VMEM((3 * RANK, length), f32)],
    )(dqkv.reshape(2, qkv_width, length), square, normed_one, inner, downs, ups, x_t, d_mixed, gain_one)

    output = swap(output, use_low, swapped)
    patch_grad = swap(patch_grad, use_low, swapped)

    up_grad = up_grad.reshape(2, 3, RANK, 3, part)
    up_grad = jnp.stack([up_grad[:, j, :, j] for j in range(3)])
    grads = jnp.stack([
        down_grad.reshape(3, RANK, width).transpose(1, 0, 2).reshape(RANK, 3 * width),
        up_grad.transpose(2, 0, 1, 3).reshape(RANK, 3 * width),
    ])
    if adapter.shape[1] % RANK == 0:
        grads = grads.reshape(2, RANK, devices, own).transpose(2, 0, 1, 3)
        summed = scatter_sum(grads).transpose(0, 2, 1).reshape(2, own * RANK)
    else:
        grads = grads.transpose(0, 2, 1).reshape(2, devices, adapter.shape[1]).transpose(1, 0, 2)
        summed = scatter_sum(grads)

    adapter_grad = summed / math.sqrt(lax.axis_size("rows") * lax.axis_size("tp") * length)
    new_mean = beta_one * adapter_mean + (1.0 - beta_one) * adapter_grad
    new_square = beta_two * adapter_square + (1.0 - beta_two) * adapter_grad * adapter_grad
    fixed_mean = new_mean / (1.0 - beta_one**adam_step)
    fixed_square = new_square / (1.0 - beta_two**adam_step)
    new_adapter = adapter - learn_rate * (
        fixed_mean / (jnp.sqrt(fixed_square) + adam_eps) + decay_rate * adapter
    )
    return (output[None], patch_grad[None], adapter_grad, new_adapter, new_mean, new_square)


def solution(mesh):
    in_specs = (
        P("rows", "tp", None),
        P("rows", None),
        P(),
        P(),
        P(None, "rows", "tp"),
        P("rows", "tp"),
        P("rows", "tp"),
        P("rows", "tp"),
        P(None, ("tp", "rows")),
        P(None, ("tp", "rows")),
        P(None, ("tp", "rows")),
        P("rows", "tp", None),
    )
    out_specs = (
        P("rows", "tp", None),
        P("rows", "tp", None),
        P(None, ("tp", "rows")),
        P(None, ("tp", "rows")),
        P(None, ("tp", "rows")),
        P(None, ("tp", "rows")),
    )
    return jax.shard_map(shards, mesh=mesh, in_specs=in_specs, out_specs=out_specs, check_vma=False)
```

time: 1860 us -> 546 us (0.29)
  waiting for transfers between devices: 869 us -> 186 us
  matrix products: 634 us -> 0 us
  Pallas kernels: 0 us -> 230 us
  other arithmetic: 214 us -> 33 us
  local copies, waits for them, and re-layouts: 70.1 us -> 24.7 us
    dot_general x60 -> x0, matrix products: 634 us -> none  [the longest x8 159 us: masked_scores(): jnp.einsum('qhd,khd->hqk', query_block, key_heads, preferred_element_type...]
    reduce_scatter x4 -> x0, waiting for transfers between devices: 312 us -> none  [the longest x1 109 us: heads_flow(): lax.psum_scatter(jnp.einsum('ch,dh->cd', piece, out_all[0], preferred_ele...]
    pallas_call x0 -> x7, Pallas kernels: none -> 230 us  [the longest x1 69.9 us: shards(): call(mlp_kernel, (2,), [whole((width, length)), whole((width, length)), b...]
    all_gather x8 -> x3, waiting for transfers between devices: 340 us -> 120 us  [the longest x1 86 us: shards(): lax.all_gather(jnp.pad(down_weight, pad), both, axis=0, tiled=True)]
    unnamed x14 -> x3, waiting for transfers between devices: 217 us -> 0.05 us
    convert_element_type x9 -> x3, other arithmetic: 123 us -> 3.63 us  [the longest x1 3.62 us: swap(): other = lax.ppermute(window.astype(bf16), 'tp', [(0, 1), (1, 0)])]
    reduce_sum x11 -> x2, other arithmetic: 76 us -> 0.72 us  [the longest x1 0.63 us: shards(): start = jnp.sum(jnp.where(lengths == length, ends - lengths, 0))]
    ppermute x0 -> x9, waiting for transfers between devices: none -> 65.8 us  [the longest x4 46.3 us: swap(): other = lax.ppermute(window.astype(bf16), 'tp', [(0, 1), (1, 0)])]
  transfers between devices with their start and end apart: 13 -> 12, of which waited for: 12 -> 10; matrix products, arithmetic and copies ran while one was open for 18% -> 8% of each run, Pallas kernels for 0% -> 13%
where the time goes in v1:
time: 546 us; the launch traced here: 542 us
  Pallas kernels  230 us (42%)
  waiting for transfers between devices  186 us (34%)
  blocking collectives  43.1 us (8%)
  other arithmetic  33 us (6%)
  local copies, waits for them, and re-layouts  24.7 us (5%)
  between operations  15.1 us (3%)
  starting transfers between devices  11 us (2%)
    all_gather x1, waiting for transfers between devices, shards(): lax.all_gather(jnp.pad(down_weight, pad), both, axis=0, tiled=True)  86 us
    pallas_call x1, Pallas kernels, shards(): call(mlp_kernel, (2,), [whole((width, length)), whole((width, length)), b...  69.9 us
    ppermute x4, waiting for transfers between devices, swap(): other = lax.ppermute(window.astype(bf16), 'tp', [(0, 1), (1, 0)])  46.3 us
    all_gather x1, blocking collectives, shards(): every = lax.all_gather(local, both, axis=0)  43.1 us
    pallas_call x1, Pallas kernels, shards(): call(attend_back_kernel, (2, heads), [table, line, head_of(0), head_of(1)...  40.4 us
    pallas_call x1, Pallas kernels, shards(): call(attend_kernel, (2, heads), [head_of(0), head_of(1), head_of(2), whol...  32.1 us
    pallas_call x1, Pallas kernels, shards(): call(functools.partial(finish_kernel, qkv_width), (2,), [by_part(qkv_widt...  30.1 us
    pallas_call x1, Pallas kernels, shards(): call(functools.partial(project_kernel, qkv_width), (2,), [whole((length,...  22.4 us
  transfers between devices with their start and end apart: 12, of which 10 were waited for; matrix products, arithmetic and copies ran while one was open for 8% of the time, Pallas kernels for 13%

profile of v1, /device:TPU:0, one launch (start us, length us, event | category | flops | bytes accessed | tf_op | source)
XLA Modules:
  0.0 542.1 jit_solution(10855627114286306256)
XLA Ops:
  8.4 1.8 concatenate.17
  15.6 2.9 collective-permute-start.1
  20.8 43.1 %all-gather = bf16[64,16,108]{2,1,0:T(8,128)(2,1)S(1)} all-gather(bf16[2,16,108]{2,1,0:T(8,128)(2,1)S(1)} %copy.61), channel_id=2, replica_groups=mesh['tp'=2,'rows'=16] {'tp','rows'}, dimensions={0}, use_global_device_ids=true | all-gather | bytes 228096 | tf_op jit(solution)/shard_map/all_gather | solution.py:296
  68.8 18.1 %collective-permute-done = bf16[512,1152]{1,0:T(8,128)(2,1)} collective-permute-done((bf16[512,1152]{1,0:T(8,128)(2,1)}, bf16[512,1152]{1,0:T(8,128)(2,1)}, u32[]{:S(2)}, u32[]{:S(2)}) %collective-permute-start) | collective-permute-done | bytes 1179680 | tf_op jit(solution)/shard_map/ppermute | solution.py:230
  86.8 7.7 %maximum_select_fusion.1 = (bf16[1024,1152]{1,0:T(8,128)(2,1)}, bf16[1024,1152]{1,0:T(8,128)(2,1)}) fusion(bf16[512,1152]{1,0:T(8,128)(2,1)} %collective-permute-done.1, bf16[1,1024,1152]{2,1,0:T(8,128)(2,1)S(1)} %copy-done.1, pred[1024]{0:T(1024)(128)(4,1)S(1)} %fusion.2, bf16[1,1024,1152]{2,1,0:T(8,128)(2,1)} %param.12, ...), kind=kLoop, calls=%fused_computation.2 | loop fusion | flops 11796480 | bytes 11797504 | tf_op jit(solution)/shard_map/jit(_where)/select_n | solution.py:231
  94.5 21.3 %all-gather.5.cloned.1.call-done = bf16[2304,2304]{1,0:T(8,128)(2,1)} async-done(((bf16[72,2304]{1,0:T(8,128)(2,1)}), bf16[2304,2304]{1,0:T(8,128)(2,1)}) %all-gather.5.cloned.1.call-update) | async-done | bytes 10616848 | tf_op jit(solution)/shard_map/all_gather | solution.py:307
  118.0 22.4 %shard_map.163 = (bf16[2,1728,1024]{2,1,0:T(8,128)(2,1)}, bf16[1152,1024]{1,0:T(8,128)(2,1)}, bf16[1152,1024]{1,0:T(8,128)(2,1)}, bf16[48,1024]{1,0:T(8,128)(2,1)}) custom-call(bf16[1024,1152]{1,0:T(8,128)(2,1)} %get-tuple-element.66.x_ref, f32[1152,128]{1,0:T(8,128)} %broadcast_in_dim.83.gain_ref, f32[1152,128]{1,0:T(8,128)} %broadcast_in_dim.85.shift_ref, ...), custom_call_target="tpu_custom_call" | custom-call | tf_op jit(solution)/shard_map/pallas_call | solution.py:316
  141.4 32.1 %shard_map.164 = (bf16[2,8,72,1024]{3,2,1,0:T(8,128)(2,1)}, bf16[2,8,1024,1024]{3,2,1,0:T(8,128)(2,1)}, f32[2,8,1,1024]{3,2,1,0:T(1,128)}) custom-call(bf16[2,3,8,72,1024]{4,3,2,1,0:T(8,128)(2,1)} %bitcast.99, bf16[2,3,8,72,1024]{4,3,2,1,0:T(8,128)(2,1)} %bitcast.100, bf16[2,3,8,72,1024]{4,3,2,1,0:T(8,128)(2,1)} %bitcast.101, ...), custom_call_target="tpu_custom_call" | custom-call | tf_op jit(solution)/shard_map/pallas_call | solution.py:331
  175.6 15.9 %shard_map.165 = (f32[1152,1024]{1,0:T(8,128)}, bf16[1152,1024]{1,0:T(8,128)(2,1)}, bf16[1152,1024]{1,0:T(8,128)(2,1)}) custom-call(bf16[1152,1024]{1,0:T(8,128)(2,1)} %get-tuple-element.24.xt_ref, bf16[2,576,1024]{2,1,0:T(8,128)(2,1)} %bitcast.112, bf16[2,1152,2304]{2,1,0:T(8,128)(2,1)} %bitcast.106, f32[1152,128]{1,0:T(8,128)} %broadcast_in_dim.91.gain_ref, ...), custom_call_target="tpu_custom_call" | custom-call | tf_op jit(solution)/shard_map/pallas_call | solution.py:341
  191.5 12.5 %all-gather.7.cloned.1.call-done = bf16[2304,2176]{1,0:T(8,128)(2,1)} async-done(((bf16[72,2176]{1,0:T(8,128)(2,1)}), bf16[2304,2176]{1,0:T(8,128)(2,1)}) %all-gather.7.cloned.1.call-update) | async-done | bytes 10027024 | tf_op jit(solution)/shard_map/all_gather | solution.py:308
  204.0 86.0 %all-gather.9.cloned.1.call-done = bf16[2304,2176]{1,0:T(8,128)(2,1)} async-done(((bf16[72,2176]{1,0:T(8,128)(2,1)}), bf16[2304,2176]{1,0:T(8,128)(2,1)}) %all-gather.9.cloned.1.call-update) | async-done | bytes 10027024 | tf_op jit(solution)/shard_map/all_gather | solution.py:309
  290.1 69.9 %shard_map.166 = (f32[1152,1024]{1,0:T(8,128)}, f32[1152,1024]{1,0:T(8,128)}) custom-call(bf16[1152,1024]{1,0:T(8,128)(2,1)} %get-tuple-element.28.normed_ref, bf16[1152,1024]{1,0:T(8,128)(2,1)} %get-tuple-element.29.cot_ref, bf16[2,1152,2176]{2,1,0:T(8,128)(2,1)} %bitcast.110, bf16[2,1152,2176]{2,1,0:T(8,128)(2,1)} %bitcast.111), custom_call_target="tpu_custom_call" | custom-call | tf_op jit(solution)/shard_map/pallas_call | solution.py:351
  359.9 18.7 %shard_map.167 = (bf16[1024,1152]{1,0:T(8,128)(2,1)}, f32[1152,1024]{1,0:T(8,128)}, bf16[2,576,1024]{2,1,0:T(8,128)(2,1)}) custom-call(f32[1152,1024]{1,0:T(8,128)} %get-tuple-element.27.mixed_ref, f32[1152,1024]{1,0:T(8,128)} %get-tuple-element.30.out_ref, f32[1152,1024]{1,0:T(8,128)} %get-tuple-element.31.grad_ref, ...), custom_call_target="tpu_custom_call" | custom-call | tf_op jit(solution)/shard_map/pallas_call | solution.py:359
  378.6 40.4 %shard_map.168 = bf16[2,3,8,72,1024]{4,3,2,1,0:T(8,128)(2,1)} custom-call(bf16[2,8,1024,1024]{3,2,1,0:T(8,128)(2,1)} %get-tuple-element.33.probs_ref, f32[2,8,1,1024]{3,2,1,0:T(1,128)} %get-tuple-element.34.inv_ref, bf16[2,3,8,72,1024]{4,3,2,1,0:T(8,128)(2,1)} %bitcast.102, bf16[2,3,8,72,1024]{4,3,2,1,0:T(8,128)(2,1)} %bitcast.103, ...), custom_call_target="tpu_custom_call" | custom-call | tf_op jit(solution)/shard_map/pallas_call | solution.py:369
  419.1 30.1 %shard_map.169 = (f32[1024,1152]{1,0:T(8,128)}, f32[2,48,1728]{2,1,0:T(8,128)}, f32[48,1152]{1,0:T(8,128)}) custom-call(bf16[2,1728,1024]{2,1,0:T(8,128)(2,1)} %bitcast.109, bf16[2,1152,2304]{2,1,0:T(8,128)(2,1)} %bitcast.108, bf16[1152,1024]{1,0:T(8,128)(2,1)} %get-tuple-element.36.normed_ref, bf16[48,1024]{1,0:T(8,128)(2,1)} %get-tuple-element.37.inner_ref, ...), custom_call_target="tpu_custom_call" | custom-call | tf_op jit(solution)/shard_map/pallas_call | solution.py:377
  454.3 7.0 %collective-permute-done.4 = f32[16,2,16,108]{3,2,1,0:T(8,128)S(1)} collective-permute-done((f32[16,2,16,108]{3,2,1,0:T(8,128)S(1)}, f32[16,2,16,108]{3,2,1,0:T(8,128)S(1)}, u32[]{:S(2)}, u32[]{:S(2)}) %collective-permute-start.4) | collective-permute-done | bytes 221216 | tf_op jit(solution)/shard_map/ppermute | solution.py:240
  461.5 1.9 collective-permute-start.5
  463.4 6.7 %collective-permute-done.5 = f32[8,2,16,108]{3,2,1,0:T(8,128)S(1)} collective-permute-done((f32[8,2,16,108]{3,2,1,0:T(8,128)S(1)}, f32[8,2,16,108]{3,2,1,0:T(8,128)S(1)}, u32[]{:S(2)}, u32[]{:S(2)}) %collective-permute-start.5) | collective-permute-done | bytes 110624 | tf_op jit(solution)/shard_map/ppermute | solution.py:240
  470.3 4.2 collective-permute-done.6
  483.5 3.6 select_convert_fusion
  496.2 11.5 %collective-permute-done.2 = bf16[512,1152]{1,0:T(8,128)(2,1)S(1)} collective-permute-done((bf16[512,1152]{1,0:T(8,128)(2,1)}, bf16[512,1152]{1,0:T(8,128)(2,1)S(1)}, u32[]{:S(2)}, u32[]{:S(2)}) %collective-permute-start.2) | collective-permute-done | bytes 1179680 | tf_op jit(solution)/shard_map/ppermute | solution.py:230
  507.7 5.3 fusion
  513.0 16.8 %collective-permute-done.3 = bf16[512,1152]{1,0:T(8,128)(2,1)} collective-permute-done((bf16[512,1152]{1,0:T(8,128)(2,1)}, bf16[512,1152]{1,0:T(8,128)(2,1)}, u32[]{:S(2)}, u32[]{:S(2)}) %collective-permute-start.3) | collective-permute-done | bytes 1179680 | tf_op jit(solution)/shard_map/ppermute | solution.py:230
  529.7 5.7 %select_bitcast_fusion = f32[1,1024,1152]{2,1,0:T(8,128)} fusion(f32[1024,1152]{1,0:T(8,128)} %get-tuple-element.39, bf16[512,1152]{1,0:T(8,128)(2,1)} %collective-permute-done.3, pred[1024]{0:T(1024)(128)(4,1)S(1)} %copy-done.8), kind=kLoop, calls=%fused_computation | loop fusion | flops 5898240 | bytes 10617856 | tf_op jit(solution)/shard_map/broadcast_in_dim | solution.py:412
  (99 shorter events, 41.4 us)
Async XLA Ops:
  7.2 5.0 copy-start.3
  7.2 5.7 %copy-start.11 = (s32[1,4]{1,0:T(1,128)S(1)}, s32[1,4]{1,0:T(1,128)}, u32[]{:S(2)}) copy-start(s32[1,4]{1,0:T(1,128)} %param.13) | copy-start | bytes 52
  7.2 7.2 %copy-start.1 = (bf16[1,1024,1152]{2,1,0:T(8,128)(2,1)S(1)}, bf16[1,1024,1152]{2,1,0:T(8,128)(2,1)}, u32[]{:S(2)}) copy-start(bf16[1,1024,1152]{2,1,0:T(8,128)(2,1)} %param.23) | copy-start | bytes 7077892
  7.2 108.6 %all-gather.5.cloned.1.call-start = ((), (), s32[]{:S(2)}) async-start(), calls=%async_computation | async-start | bytes 10948608 | tf_op jit(solution)/shard_map/all_gather | solution.py:307
  10.3 193.8 %all-gather.7.cloned.1.call-start = ((), (), s32[]{:S(2)}) async-start(), calls=%async_computation.1 | async-start | bytes 10340352 | tf_op jit(solution)/shard_map/all_gather | solution.py:308
  12.1 278.0 %all-gather.9.cloned.1.call-start = ((), (), s32[]{:S(2)}) async-start(), calls=%async_computation.2 | async-start | bytes 10340352 | tf_op jit(solution)/shard_map/all_gather | solution.py:309
  14.4 4.1 copy-start.2
  15.6 5.0 copy-start.5
  15.6 53.2 %collective-permute-start.1 = (bf16[512,1152]{1,0:T(8,128)(2,1)}, bf16[512,1152]{1,0:T(8,128)(2,1)}, u32[]{:S(2)}, u32[]{:S(2)}) collective-permute-start(bf16[512,1152]{1,0:T(8,128)(2,1)} %select_bitcast_fusion.1), channel_id=1, source_target_pairs={{0,16},{16,0},{1,17},{17,1},{2,18},{18,2},{3,19},{19,3},{4,20},{20... | collective-permute-start | bytes 3538952 | tf_op jit(solution)/shard_map/ppermute | solution.py:230
  19.6 67.2 %collective-permute-start = (bf16[512,1152]{1,0:T(8,128)(2,1)}, bf16[512,1152]{1,0:T(8,128)(2,1)}, u32[]{:S(2)}, u32[]{:S(2)}) collective-permute-start(bf16[512,1152]{1,0:T(8,128)(2,1)} %select_bitcast_fusion.2), channel_id=1, source_target_pairs={{0,16},{16,0},{1,17},{17,1},{2,18},{18,2},{3,19},{19,3},{4,20},{20... | collective-permute-start | bytes 3538952 | tf_op jit(solution)/shard_map/ppermute | solution.py:230
  63.9 3.9 copy-start.9
  63.9 4.0 copy-start.10
  67.1 27.4 %copy-start.7 = (pred[1024]{0:T(1024)(128)(4,1)}, pred[1024]{0:T(1024)(128)(4,1)S(1)}, u32[]{:S(2)}) copy-start(pred[1024]{0:T(1024)(128)(4,1)S(1)} %fusion.2) | copy-start | bytes 3076
  68.0 72.4 %copy-start.6 = (s32[1024]{0:T(1024)}, s32[1024]{0:T(1024)S(1)}, u32[]{:S(2)}) copy-start(s32[1024]{0:T(1024)S(1)} %convert_reduce_fusion) | copy-start | bytes 12292
  449.2 2.9 copy-start.4
  452.6 24.8 %copy-start = (bf16[1024,1152]{1,0:T(8,128)(2,1)S(1)}, bf16[1024,1152]{1,0:T(8,128)(2,1)}, u32[]{:S(2)}) copy-start(bf16[1024,1152]{1,0:T(8,128)(2,1)} %get-tuple-element.32) | copy-start | bytes 7077892
  452.8 8.5 %collective-permute-start.4 = (f32[16,2,16,108]{3,2,1,0:T(8,128)S(1)}, f32[16,2,16,108]{3,2,1,0:T(8,128)S(1)}, u32[]{:S(2)}, u32[]{:S(2)}) collective-permute-start(f32[16,2,16,108]{3,2,1,0:T(8,128)S(1)} %bitcast.127), channel_id=1, source_target_pairs={{0,16},{16,0},{1,17},{17,1},{2,18},{18,2},{3,19},{19,3},{4,20},{20... | collective-permute-start | bytes 663560 | tf_op jit(solution)/shard_map/ppermute | solution.py:240
  461.5 8.6 %collective-permute-start.5 = (f32[8,2,16,108]{3,2,1,0:T(8,128)S(1)}, f32[8,2,16,108]{3,2,1,0:T(8,128)S(1)}, u32[]{:S(2)}, u32[]{:S(2)}) collective-permute-start(f32[8,2,16,108]{3,2,1,0:T(8,128)S(1)} %dynamic-slice_bitcast_fusion), channel_id=1, source_target_pairs={{0,8},{1,9},{2,10},{3,11},{4,12},{5,13},{6,14},{7,15},{8,0},{9,1},... | collective-permute-start | bytes 331784 | tf_op jit(solution)/shard_map/ppermute | solution.py:240
  470.1 4.3 collective-permute-start.6
  475.9 6.3 %collective-permute-start.7 = (f32[2,2,16,108]{2,3,1,0:T(8,128)}, f32[2,2,16,108]{2,3,1,0:T(8,128)}, u32[]{:S(2)}, u32[]{:S(2)}) collective-permute-start(f32[2,2,16,108]{2,3,1,0:T(8,128)} %bitcast.45), channel_id=1, source_target_pairs={{0,2},{1,3},{2,0},{3,1},{4,6},{5,7},{6,4},{7,5},{8,10},{9,11},{10,... | collective-permute-start | bytes 82952 | tf_op jit(solution)/shard_map/ppermute | solution.py:240
  478.6 29.1 %collective-permute-start.2 = (bf16[512,1152]{1,0:T(8,128)(2,1)}, bf16[512,1152]{1,0:T(8,128)(2,1)S(1)}, u32[]{:S(2)}, u32[]{:S(2)}) collective-permute-start(bf16[512,1152]{1,0:T(8,128)(2,1)} %slice_select_fusion), channel_id=1, source_target_pairs={{0,16},{16,0},{1,17},{17,1},{2,18},{18,2},{3,19},{19,3},{4,20},{20... | collective-permute-start | bytes 3538952 | tf_op jit(solution)/shard_map/ppermute | solution.py:230
  483.4 5.1 collective-permute-start.8
  487.1 42.6 %collective-permute-start.3 = (bf16[512,1152]{1,0:T(8,128)(2,1)}, bf16[512,1152]{1,0:T(8,128)(2,1)}, u32[]{:S(2)}, u32[]{:S(2)}) collective-permute-start(bf16[512,1152]{1,0:T(8,128)(2,1)} %select_convert_fusion), channel_id=1, source_target_pairs={{0,16},{16,0},{1,17},{17,1},{2,18},{18,2},{3,19},{19,3},{4,20},{20... | collective-permute-start | bytes 3538952 | tf_op jit(solution)/shard_map/ppermute | solution.py:230
  496.2 33.6 %copy-start.8 = (pred[1024]{0:T(1024)(128)(4,1)S(1)}, pred[1024]{0:T(1024)(128)(4,1)}, u32[]{:S(2)}) copy-start(pred[1024]{0:T(1024)(128)(4,1)} %copy-done.7) | copy-start | bytes 3076
Sparse Core Ops, SparseCore 0:
  10.9 104.8 all-gather.4
  118.7 85.3 all-gather.6
  206.9 83.1 all-gather.8
